TPU v7x, 32 devices: a whole 2x2x4 slice. The times are simulated.
32 devices in a mesh: along: 2 (over core), across: 4 (over y, x), chan: 4 (over z).
Axes of the slice: x: 2, y: 2, z: 4, core: 2. Of those that a mesh axis runs over, the one named last changes fastest.
Arguments:
- jacobian: float32 [8, 32, 512, 384], P('along', 'across', 'chan'), may hold values from -0.3125 to 0.3125
- departures: float32 [8, 32, 512], P('along', 'across', 'chan'), may hold values from -6 to 6
- inv_variance: float32 [512], P('chan'), may hold values from 0.3 to 3
- channel_use: int32 [512], P('chan'), may hold values 0 or 1
- clear_flags: int32 [8, 32], P('along', 'across'), may hold values 0 or 1
- coefficients: float32 [25, 384], replicated, may hold values from -1.25 to 1.25
Outputs:
- control: float32 [8, 32, 384], P('along', 'across')
- increment: float32 [8, 32, 384], P('along', 'across')
- residual: float32 [8, 32, 384], P('along', 'across')
All inputs are finite; a program needn't handle non-finite values. No bound on the sum of `channel_use` or of `clear_flags` on one device may be relied on, other than what follows from the above.
Results may differ from a plain program's by a relative error of at most 0.0003.
Values sent between devices are 32-bit elements; how exact they have to be, the bound alone decides.
A program may use at most 64 MiB of HBM per device.

v0:
```python
import jax
import jax.numpy as jnp
from jax import lax
from jax.sharding import PartitionSpec as P

ITERS = 10


def extended(cells, sides, width):
    for axis, dim in sides:
        count = lax.axis_size(axis)
        ends = count - 1
        head = lax.slice_in_dim(cells, 0, width, axis=dim)
        tail = lax.slice_in_dim(cells, cells.shape[dim] - width, cells.shape[dim], axis=dim)
        cells = jnp.concatenate(
            [
                lax.ppermute(tail, axis, [(i, (i + 1) % count) for i in range(ends)]),
                cells,
                lax.ppermute(head, axis, [((i + 1) % count, i) for i in range(ends)]),
            ],
            axis=dim,
        )
    return cells


def widen_rim(field):
    return extended(field, (("along", 0), ("across", 1)), 2)


def spread(field, local_coef):
    rows_here, cols_here = (field.shape[0], field.shape[1])
    padded = widen_rim(field)
    result = jnp.zeros(field.shape, jnp.float32)
    for row_shift in range(5):
        for col_shift in range(5):
            result = (
                result
                + local_coef[row_shift * 5 + col_shift]
                * padded[row_shift : row_shift + rows_here, col_shift : col_shift + cols_here]
            )
    return result


def spread_back(field, local_coef):
    rows_here, cols_here = (field.shape[0], field.shape[1])
    padded = widen_rim(field)
    result = jnp.zeros(field.shape, jnp.float32)
    for row_shift in range(5):
        for col_shift in range(5):
            result = (
                result
                + local_coef[row_shift * 5 + col_shift]
                * padded[
                    4 - row_shift : 4 - row_shift + rows_here,
                    4 - col_shift : 4 - col_shift + cols_here,
                ]
            )
    return result


def on_device(jacobian, departures, inv_variance, channel_use, clear_flags, coefficients):
    weight = (
        inv_variance[None, None, :]
        * channel_use.astype(jnp.float32)[None, None, :]
        * clear_flags.astype(jnp.float32)[:, :, None]
    )

    def forward(field):
        return jnp.einsum("xycs,xys->xyc", jacobian, field, precision=lax.Precision.HIGHEST)

    def back_project(weighted):
        adjoint_obs = jnp.einsum(
            "xycs,xyc->xys", jacobian, weighted, precision=lax.Precision.HIGHEST
        )
        return lax.psum(adjoint_obs, "chan")

    def hessian(direction):
        return direction + spread_back(
            back_project(weight * forward(spread(direction, coefficients))), coefficients
        )

    def inner_pair(first, second, third, fourth):
        return lax.psum((jnp.sum(first * second), jnp.sum(third * fourth)), ("along", "across"))

    rhs = spread_back(back_project(weight * departures), coefficients)
    control = jnp.zeros_like(rhs)
    image = hessian(rhs)
    norm_now, product = inner_pair(rhs, rhs, rhs, image)
    alpha = norm_now / product

    def cg_step(step_index, state_tuple):
        control, residual, direction, conj_image, norm_now, alpha = state_tuple
        control = control + alpha * direction
        residual = residual - alpha * conj_image
        image = hessian(residual)
        fresh_norm, product = inner_pair(residual, residual, residual, image)
        beta_ratio = fresh_norm / norm_now
        alpha_next = fresh_norm / (product - beta_ratio * fresh_norm / alpha)
        direction = residual + beta_ratio * direction
        conj_image = image + beta_ratio * conj_image
        return (control, residual, direction, conj_image, fresh_norm, alpha_next)

    control, residual, direction, conj_image, norm_now, alpha = lax.fori_loop(
        0, ITERS - 1, cg_step, (control, rhs, rhs, image, norm_now, alpha)
    )
    control = control + alpha * direction
    residual = residual - alpha * conj_image
    increment = spread(control, coefficients)
    return (control, increment, residual)


def solution(mesh):
    return jax.shard_map(
        on_device,
        mesh=mesh,
        in_specs=(
            P("along", "across", "chan", None),
            P("along", "across", "chan"),
            P("chan"),
            P("chan"),
            P("along", "across"),
            P(),
        ),
        out_specs=(
            P("along", "across", None),
            P("along", "across", None),
            P("along", "across", None),
        ),
        check_vma=False,
    )
```

profile of v0, /device:TPU:0, one launch (start us, length us, event | category | flops | bytes accessed | tf_op | source)
XLA Modules:
  0.0 830.2 jit_solution(16266260684753608233)
XLA Ops:
  2.8 5.8 fusion.298
  8.6 21.3 %psum.49 = f32[4,8,384]{2,1,0:T(8,128)S(1)} all-reduce(f32[4,8,384]{2,1,0:T(8,128)S(1)} %bitcast.53), channel_id=1, replica_groups=mesh['along'=2,'across'=4,'chan'=4] {'chan'}, use_global_device_ids=true, to_apply=%region_0.0 | all-reduce | flops 12288 | bytes 98304 | tf_op jit(solution)/shard_map/psum | solution.py:75
  52.1 5.6 collective-permute-done.15
  57.9 8.7 %fusion.284 = f32[4,8,1,128]{3,2,1,0:T(1,128)S(1)} fusion(f32[4,8,128,384]{3,2,1,0:T(8,128)} %param.8, f32[4,8,384,1]{2,1,0,3:T(8,128)S(1)} %fusion.135), kind=kOutput, calls=%fused_computation.537 | convolution fusion | flops 18874368 | bytes 6356992 | tf_op jit(solution)/shard_map/xycs,xys->xyc/dot_general | solution.py:69
  70.4 16.2 %psum.50 = f32[4,8,384]{2,1,0:T(8,128)S(1)} all-reduce(f32[4,8,384]{2,1,0:T(8,128)S(1)} %bitcast.54), channel_id=1, replica_groups=mesh['along'=2,'across'=4,'chan'=4] {'chan'}, use_global_device_ids=true, to_apply=%region_1.0 | all-reduce | flops 12288 | bytes 98304 | tf_op jit(solution)/shard_map/psum | solution.py:75
  92.3 5.3 collective-permute-start.19
  99.9 17.4 %all-reduce.1 = (f32[]{:T(128)}, f32[]{:T(128)}) all-reduce(f32[]{:T(128)} %get-tuple-element.132, f32[]{:T(128)} %get-tuple-element.131), channel_id=1, replica_groups=mesh['along'=2,'across'=4,'chan'=4] {'along','across'}, use_global_device_ids=true, to_apply=%region_3.0 | all-reduce | flops 2 | bytes 16 | tf_op jit(solution)/shard_map/psum | solution.py:83
  118.6 697.0 %while.21 = (s32[]{:T(128)}, f32[4,8,384]{2,1,0:T(8,128)S(1)}, f32[4,8,384]{2,1,0:T(8,128)S(1)}, f32[4,8,384]{2,1,0:T(8,128)S(1)}, f32[4,8,384]{2,1,0:T(8,128)S(...) while((s32[]{:T(128)}, f32[4,8,384]{2,1,0:T(8,128)S(1)}, ...), condition=%wide.region_12.0_spmd.clone, body=%wide.region_6.0_spmd.clone.sunk | while | flops 39649280 | bytes 42392784 | solution.py:103
  134.2 8.7 %fusion.324 = f32[4,8,1,128]{3,2,1,0:T(1,128)S(1)} fusion(f32[4,8,128,384]{3,2,1,0:T(8,128)} %get-tuple-element.441, f32[4,8,384,1]{2,1,0,3:T(8,128)S(1)} %fusion.323), kind=kOutput, calls=%fused_computation.166.clone.1 | convolution fusion | flops 18874368 | bytes 6356992 | tf_op jit(solution)/shard_map/while/body/eval_jaxpr/xycs,xys->xyc/dot_general | solution.py:69
  146.7 17.9 %psum.57 = f32[4,8,384]{2,1,0:T(8,128)S(1)} all-reduce(f32[4,8,384]{2,1,0:T(8,128)S(1)} %bitcast.50), channel_id=1, replica_groups=mesh['along'=2,'across'=4,'chan'=4] {'chan'}, use_global_device_ids=true, to_apply=%region_9.0 | all-reduce | flops 12288 | bytes 98304 | tf_op jit(solution)/shard_map/while/body/eval_jaxpr/psum | solution.py:75
  179.3 15.4 %all-reduce.3 = (f32[]{:T(128)}, f32[]{:T(128)}) all-reduce(f32[]{:T(128)} %get-tuple-element.399, f32[]{:T(128)} %get-tuple-element.400), channel_id=1, replica_groups=mesh['along'=2,'across'=4,'chan'=4] {'along','across'}, use_global_device_ids=true, to_apply=%region_8.0 | all-reduce | flops 2 | bytes 16 | tf_op jit(solution)/shard_map/while/body/eval_jaxpr/psum | solution.py:83
  206.8 5.4 collective-permute-done.3
  212.4 8.7 %fusion.324 = f32[4,8,1,128]{3,2,1,0:T(1,128)S(1)} fusion(f32[4,8,128,384]{3,2,1,0:T(8,128)} %get-tuple-element.441, f32[4,8,384,1]{2,1,0,3:T(8,128)S(1)} %fusion.323), kind=kOutput, calls=%fused_computation.166.clone.1 | convolution fusion | flops 18874368 | bytes 6356992 | tf_op jit(solution)/shard_map/while/body/eval_jaxpr/xycs,xys->xyc/dot_general | solution.py:69
  224.8 16.5 %psum.57 = f32[4,8,384]{2,1,0:T(8,128)S(1)} all-reduce(f32[4,8,384]{2,1,0:T(8,128)S(1)} %bitcast.50), channel_id=1, replica_groups=mesh['along'=2,'across'=4,'chan'=4] {'chan'}, use_global_device_ids=true, to_apply=%region_9.0 | all-reduce | flops 12288 | bytes 98304 | tf_op jit(solution)/shard_map/while/body/eval_jaxpr/psum | solution.py:75
  256.8 14.3 %all-reduce.3 = (f32[]{:T(128)}, f32[]{:T(128)}) all-reduce(f32[]{:T(128)} %get-tuple-element.399, f32[]{:T(128)} %get-tuple-element.400), channel_id=1, replica_groups=mesh['along'=2,'across'=4,'chan'=4] {'along','across'}, use_global_device_ids=true, to_apply=%region_8.0 | all-reduce | flops 2 | bytes 16 | tf_op jit(solution)/shard_map/while/body/eval_jaxpr/psum | solution.py:83
  283.8 4.9 collective-permute-done.3
  288.9 8.7 %fusion.324 = f32[4,8,1,128]{3,2,1,0:T(1,128)S(1)} fusion(f32[4,8,128,384]{3,2,1,0:T(8,128)} %get-tuple-element.441, f32[4,8,384,1]{2,1,0,3:T(8,128)S(1)} %fusion.323), kind=kOutput, calls=%fused_computation.166.clone.1 | convolution fusion | flops 18874368 | bytes 6356992 | tf_op jit(solution)/shard_map/while/body/eval_jaxpr/xycs,xys->xyc/dot_general | solution.py:69
  301.3 17.8 %psum.57 = f32[4,8,384]{2,1,0:T(8,128)S(1)} all-reduce(f32[4,8,384]{2,1,0:T(8,128)S(1)} %bitcast.50), channel_id=1, replica_groups=mesh['along'=2,'across'=4,'chan'=4] {'chan'}, use_global_device_ids=true, to_apply=%region_9.0 | all-reduce | flops 12288 | bytes 98304 | tf_op jit(solution)/shard_map/while/body/eval_jaxpr/psum | solution.py:75
  323.6 4.8 collective-permute-start.6
  334.9 14.3 %all-reduce.3 = (f32[]{:T(128)}, f32[]{:T(128)}) all-reduce(f32[]{:T(128)} %get-tuple-element.399, f32[]{:T(128)} %get-tuple-element.400), channel_id=1, replica_groups=mesh['along'=2,'across'=4,'chan'=4] {'along','across'}, use_global_device_ids=true, to_apply=%region_8.0 | all-reduce | flops 2 | bytes 16 | tf_op jit(solution)/shard_map/while/body/eval_jaxpr/psum | solution.py:83
  361.9 4.9 collective-permute-done.3
  367.0 8.7 %fusion.324 = f32[4,8,1,128]{3,2,1,0:T(1,128)S(1)} fusion(f32[4,8,128,384]{3,2,1,0:T(8,128)} %get-tuple-element.441, f32[4,8,384,1]{2,1,0,3:T(8,128)S(1)} %fusion.323), kind=kOutput, calls=%fused_computation.166.clone.1 | convolution fusion | flops 18874368 | bytes 6356992 | tf_op jit(solution)/shard_map/while/body/eval_jaxpr/xycs,xys->xyc/dot_general | solution.py:69
  379.4 16.5 %psum.57 = f32[4,8,384]{2,1,0:T(8,128)S(1)} all-reduce(f32[4,8,384]{2,1,0:T(8,128)S(1)} %bitcast.50), channel_id=1, replica_groups=mesh['along'=2,'across'=4,'chan'=4] {'chan'}, use_global_device_ids=true, to_apply=%region_9.0 | all-reduce | flops 12288 | bytes 98304 | tf_op jit(solution)/shard_map/while/body/eval_jaxpr/psum | solution.py:75
  400.3 4.6 collective-permute-start.6
  411.4 14.3 %all-reduce.3 = (f32[]{:T(128)}, f32[]{:T(128)}) all-reduce(f32[]{:T(128)} %get-tuple-element.399, f32[]{:T(128)} %get-tuple-element.400), channel_id=1, replica_groups=mesh['along'=2,'across'=4,'chan'=4] {'along','across'}, use_global_device_ids=true, to_apply=%region_8.0 | all-reduce | flops 2 | bytes 16 | tf_op jit(solution)/shard_map/while/body/eval_jaxpr/psum | solution.py:83
  438.4 4.9 collective-permute-done.3
  443.5 8.7 %fusion.324 = f32[4,8,1,128]{3,2,1,0:T(1,128)S(1)} fusion(f32[4,8,128,384]{3,2,1,0:T(8,128)} %get-tuple-element.441, f32[4,8,384,1]{2,1,0,3:T(8,128)S(1)} %fusion.323), kind=kOutput, calls=%fused_computation.166.clone.1 | convolution fusion | flops 18874368 | bytes 6356992 | tf_op jit(solution)/shard_map/while/body/eval_jaxpr/xycs,xys->xyc/dot_general | solution.py:69
  455.9 17.8 %psum.57 = f32[4,8,384]{2,1,0:T(8,128)S(1)} all-reduce(f32[4,8,384]{2,1,0:T(8,128)S(1)} %bitcast.50), channel_id=1, replica_groups=mesh['along'=2,'across'=4,'chan'=4] {'chan'}, use_global_device_ids=true, to_apply=%region_9.0 | all-reduce | flops 12288 | bytes 98304 | tf_op jit(solution)/shard_map/while/body/eval_jaxpr/psum | solution.py:75
  478.1 4.8 collective-permute-start.6
  489.5 14.3 %all-reduce.3 = (f32[]{:T(128)}, f32[]{:T(128)}) all-reduce(f32[]{:T(128)} %get-tuple-element.399, f32[]{:T(128)} %get-tuple-element.400), channel_id=1, replica_groups=mesh['along'=2,'across'=4,'chan'=4] {'along','across'}, use_global_device_ids=true, to_apply=%region_8.0 | all-reduce | flops 2 | bytes 16 | tf_op jit(solution)/shard_map/while/body/eval_jaxpr/psum | solution.py:83
  516.4 4.9 collective-permute-done.3
  521.5 8.7 %fusion.324 = f32[4,8,1,128]{3,2,1,0:T(1,128)S(1)} fusion(f32[4,8,128,384]{3,2,1,0:T(8,128)} %get-tuple-element.441, f32[4,8,384,1]{2,1,0,3:T(8,128)S(1)} %fusion.323), kind=kOutput, calls=%fused_computation.166.clone.1 | convolution fusion | flops 18874368 | bytes 6356992 | tf_op jit(solution)/shard_map/while/body/eval_jaxpr/xycs,xys->xyc/dot_general | solution.py:69
  534.0 16.5 %psum.57 = f32[4,8,384]{2,1,0:T(8,128)S(1)} all-reduce(f32[4,8,384]{2,1,0:T(8,128)S(1)} %bitcast.50), channel_id=1, replica_groups=mesh['along'=2,'across'=4,'chan'=4] {'chan'}, use_global_device_ids=true, to_apply=%region_9.0 | all-reduce | flops 12288 | bytes 98304 | tf_op jit(solution)/shard_map/while/body/eval_jaxpr/psum | solution.py:75
  566.0 14.3 %all-reduce.3 = (f32[]{:T(128)}, f32[]{:T(128)}) all-reduce(f32[]{:T(128)} %get-tuple-element.399, f32[]{:T(128)} %get-tuple-element.400), channel_id=1, replica_groups=mesh['along'=2,'across'=4,'chan'=4] {'along','across'}, use_global_device_ids=true, to_apply=%region_8.0 | all-reduce | flops 2 | bytes 16 | tf_op jit(solution)/shard_map/while/body/eval_jaxpr/psum | solution.py:83
  592.9 4.9 collective-permute-done.3
  598.0 8.7 %fusion.324 = f32[4,8,1,128]{3,2,1,0:T(1,128)S(1)} fusion(f32[4,8,128,384]{3,2,1,0:T(8,128)} %get-tuple-element.441, f32[4,8,384,1]{2,1,0,3:T(8,128)S(1)} %fusion.323), kind=kOutput, calls=%fused_computation.166.clone.1 | convolution fusion | flops 18874368 | bytes 6356992 | tf_op jit(solution)/shard_map/while/body/eval_jaxpr/xycs,xys->xyc/dot_general | solution.py:69
  610.5 17.8 %psum.57 = f32[4,8,384]{2,1,0:T(8,128)S(1)} all-reduce(f32[4,8,384]{2,1,0:T(8,128)S(1)} %bitcast.50), channel_id=1, replica_groups=mesh['along'=2,'across'=4,'chan'=4] {'chan'}, use_global_device_ids=true, to_apply=%region_9.0 | all-reduce | flops 12288 | bytes 98304 | tf_op jit(solution)/shard_map/while/body/eval_jaxpr/psum | solution.py:75
  632.7 4.8 collective-permute-start.6
  644.0 14.3 %all-reduce.3 = (f32[]{:T(128)}, f32[]{:T(128)}) all-reduce(f32[]{:T(128)} %get-tuple-element.399, f32[]{:T(128)} %get-tuple-element.400), channel_id=1, replica_groups=mesh['along'=2,'across'=4,'chan'=4] {'along','across'}, use_global_device_ids=true, to_apply=%region_8.0 | all-reduce | flops 2 | bytes 16 | tf_op jit(solution)/shard_map/while/body/eval_jaxpr/psum | solution.py:83
  671.0 4.9 collective-permute-done.3
  676.1 8.7 %fusion.324 = f32[4,8,1,128]{3,2,1,0:T(1,128)S(1)} fusion(f32[4,8,128,384]{3,2,1,0:T(8,128)} %get-tuple-element.441, f32[4,8,384,1]{2,1,0,3:T(8,128)S(1)} %fusion.323), kind=kOutput, calls=%fused_computation.166.clone.1 | convolution fusion | flops 18874368 | bytes 6356992 | tf_op jit(solution)/shard_map/while/body/eval_jaxpr/xycs,xys->xyc/dot_general | solution.py:69
  688.5 16.5 %psum.57 = f32[4,8,384]{2,1,0:T(8,128)S(1)} all-reduce(f32[4,8,384]{2,1,0:T(8,128)S(1)} %bitcast.50), channel_id=1, replica_groups=mesh['along'=2,'across'=4,'chan'=4] {'chan'}, use_global_device_ids=true, to_apply=%region_9.0 | all-reduce | flops 12288 | bytes 98304 | tf_op jit(solution)/shard_map/while/body/eval_jaxpr/psum | solution.py:75
  720.5 14.3 %all-reduce.3 = (f32[]{:T(128)}, f32[]{:T(128)}) all-reduce(f32[]{:T(128)} %get-tuple-element.399, f32[]{:T(128)} %get-tuple-element.400), channel_id=1, replica_groups=mesh['along'=2,'across'=4,'chan'=4] {'along','across'}, use_global_device_ids=true, to_apply=%region_8.0 | all-reduce | flops 2 | bytes 16 | tf_op jit(solution)/shard_map/while/body/eval_jaxpr/psum | solution.py:83
  747.5 4.9 collective-permute-done.3
  752.6 8.7 %fusion.324 = f32[4,8,1,128]{3,2,1,0:T(1,128)S(1)} fusion(f32[4,8,128,384]{3,2,1,0:T(8,128)} %get-tuple-element.441, f32[4,8,384,1]{2,1,0,3:T(8,128)S(1)} %fusion.323), kind=kOutput, calls=%fused_computation.166.clone.1 | convolution fusion | flops 18874368 | bytes 6356992 | tf_op jit(solution)/shard_map/while/body/eval_jaxpr/xycs,xys->xyc/dot_general | solution.py:69
  765.1 17.8 %psum.57 = f32[4,8,384]{2,1,0:T(8,128)S(1)} all-reduce(f32[4,8,384]{2,1,0:T(8,128)S(1)} %bitcast.50), channel_id=1, replica_groups=mesh['along'=2,'across'=4,'chan'=4] {'chan'}, use_global_device_ids=true, to_apply=%region_9.0 | all-reduce | flops 12288 | bytes 98304 | tf_op jit(solution)/shard_map/while/body/eval_jaxpr/psum | solution.py:75
  787.3 4.8 collective-permute-start.6
  798.6 14.3 %all-reduce.3 = (f32[]{:T(128)}, f32[]{:T(128)}) all-reduce(f32[]{:T(128)} %get-tuple-element.399, f32[]{:T(128)} %get-tuple-element.400), channel_id=1, replica_groups=mesh['along'=2,'across'=4,'chan'=4] {'along','across'}, use_global_device_ids=true, to_apply=%region_8.0 | all-reduce | flops 2 | bytes 16 | tf_op jit(solution)/shard_map/while/body/eval_jaxpr/psum | solution.py:83
  (374 shorter events, 289.4 us)
Async XLA Ops:
  34.3 5.9 collective-permute-start.10
  35.6 6.1 collective-permute-start.11
  46.3 5.9 collective-permute-start.14
  50.6 7.2 collective-permute-start.15
  91.0 6.7 collective-permute-start.18
  92.3 6.8 collective-permute-start.19
  118.7 4.7 collective-permute-start
  124.1 5.7 collective-permute-start.2
  128.3 5.7 collective-permute-start.3
  169.0 5.7 collective-permute-start.6
  172.8 5.7 collective-permute-start.7
  197.4 4.8 collective-permute-start
  205.3 6.9 collective-permute-start.3
  245.7 6.5 collective-permute-start.6
  250.3 5.7 collective-permute-start.7
  273.9 4.8 collective-permute-start
  279.5 4.3 collective-permute-start.2
  282.3 6.4 collective-permute-start.3
  323.6 6.8 collective-permute-start.6
  328.4 5.7 collective-permute-start.7
  352.0 4.8 collective-permute-start
  357.5 4.3 collective-permute-start.2
  360.3 6.4 collective-permute-start.3
  400.3 6.5 collective-permute-start.6
  404.9 5.7 collective-permute-start.7
  428.5 4.8 collective-permute-start
  434.1 4.3 collective-permute-start.2
  436.9 6.4 collective-permute-start.3
  478.1 6.8 collective-permute-start.6
  482.9 5.7 collective-permute-start.7
  506.5 4.8 collective-permute-start
  512.1 4.3 collective-permute-start.2
  514.9 6.4 collective-permute-start.3
  554.9 6.5 collective-permute-start.6
  559.5 5.7 collective-permute-start.7
  583.0 4.8 collective-permute-start
  591.4 6.4 collective-permute-start.3
  632.7 6.8 collective-permute-start.6
  637.5 5.7 collective-permute-start.7
  661.1 4.8 collective-permute-start
  669.5 6.4 collective-permute-start.3
  709.4 6.5 collective-permute-start.6
  714.0 5.7 collective-permute-start.7
  737.6 4.8 collective-permute-start
  746.0 6.4 collective-permute-start.3
  787.3 6.8 collective-permute-start.6
  792.1 5.7 collective-permute-start.7
  823.0 6.4 collective-permute-start.23
  (53 other events, 473.4 us)
where the time goes:
time: 833 us; the launch traced here: 830 us
  blocking collectives  340 us (41%)
  starting transfers between devices  189 us (23%)
  matrix products  129 us (15%)
  waiting for transfers between devices  122 us (15%)
  loops' own time  31.3 us (4%)
  other arithmetic  14.8 us (2%)
    psum x11, blocking collectives, back_project(): return lax.psum(adjoint_obs, 'chan')  192 us
    psum x10, blocking collectives, inner_pair(): lax.psum((jnp.sum(first * second), jnp.sum(third * fourth)), ('along', 'a...  147 us
    ppermute x44, starting transfers between devices, extended(): lax.ppermute(tail, axis, [(i, (i + 1) % count) for i in range(ends)])  130 us
    ppermute x44, waiting for transfers between devices, extended(): lax.ppermute(head, axis, [((i + 1) % count, i) for i in range(ends)])  111 us
    dot_general x10, matrix products, forward(): jnp.einsum('xycs,xys->xyc', jacobian, field, precision=lax.Precision.HIGH...  87.2 us
    ppermute x44, starting transfers between devices, extended(): lax.ppermute(head, axis, [((i + 1) % count, i) for i in range(ends)])  59.5 us
    dot_general x11, matrix products, back_project(): jnp.einsum('xycs,xyc->xys', jacobian, weighted, precision=lax.Precision.H...  42.1 us
    another operation x1, loops' own time, on_device(): lax.fori_loop(0, ITERS - 1, cg_step, (control, rhs, rhs, image, norm_now,...  31.3 us
  transfers between devices with their start and end apart: 88, of which 53 were waited for; matrix products, arithmetic and copies ran while one was open for 0% of the time, Pallas kernels for 0%

commit v1 on v0

v1 whole, which is shorter than its diff:
```python
import functools

import jax
import jax.numpy as jnp
from jax import lax
from jax.experimental import pallas as pl
from jax.experimental.pallas import tpu as pltpu
from jax.sharding import PartitionSpec as P

ITERS = 10
RIM = 2
WIDE = 2 * RIM
TAPS = 2 * RIM + 1
PACK = 4
MESH = pl.DeviceIdType.MESH


def kernel(
    dims, jac_hbm, dep_ref, var_ref, use_ref, flag_ref, coef_ref,
    ctl_ref, inc_ref, res_ref,
    jac, wt, coef, part, wide, sums, urs, fr, fd, fc, fx, keep,
    jac_sem, chan_send, chan_recv, rim_send, rim_recv, sum_send, sum_recv,
):
    n_along, n_across, n_chan = dims
    rows, cols, chans, _ = jac.shape
    lanes = part.shape[-1]
    tiles = coef_ref.shape[1] // lanes
    ext_r, ext_c = rows + 2 * RIM, cols + 2 * RIM
    group = n_along * n_across
    f32 = jnp.float32

    a_me = lax.axis_index("along")
    x_me = lax.axis_index("across")
    c_me = lax.axis_index("chan")
    g_me = a_me * n_across + x_me

    loads = [
        pltpu.make_async_copy(jac_hbm.at[i], jac.at[i], jac_sem.at[i]) for i in range(rows)
    ]
    for load in loads:
        load.start()

    wide[...] = jnp.zeros_like(wide)
    sums[...] = jnp.zeros_like(sums)
    urs[...] = jnp.zeros_like(urs)
    fd[...] = jnp.zeros_like(fd)
    fc[...] = jnp.zeros_like(fc)
    fx[...] = jnp.zeros_like(fx)
    coef[...] = jnp.zeros_like(coef)
    keep[...] = jnp.ones_like(keep)

    chan_peers = [lax.rem(c_me + d, n_chan) for d in range(1, n_chan)]
    group_peers = []
    for d in range(1, group):
        peer = lax.rem(g_me + d, group)
        group_peers.append((peer // n_across, lax.rem(peer, n_across)))

    barrier = pltpu.get_barrier_semaphore()
    for c in chan_peers:
        pl.semaphore_signal(barrier, inc=1, device_id={"chan": c}, device_id_type=MESH)
    for a, x in group_peers:
        pl.semaphore_signal(
            barrier, inc=1, device_id={"along": a, "across": x}, device_id_type=MESH
        )
    pl.semaphore_wait(barrier, len(chan_peers) + len(group_peers))

    for t in range(TAPS * TAPS):
        for l in range(tiles):
            row = coef_ref[t : t + 1, l * lanes : (l + 1) * lanes]
            coef[t, l : l + 1, :] = row
            coef[t, PACK + l : PACK + l + 1, :] = row

    chan_weight = var_ref[...] * use_ref[...].astype(f32)
    wd = dep_ref[...].reshape(rows * cols, chans) * chan_weight
    stack = jnp.concatenate([wd, jnp.broadcast_to(chan_weight, (8, chans))], axis=0)
    turned = jnp.transpose(stack)
    blocks = chans // 8
    for k in range(blocks):
        wt[k] = jnp.broadcast_to(
            turned[k * 8 : (k + 1) * 8, rows * cols : rows * cols + 1], (8, lanes)
        )

    def chan_copy(par, i, d):
        place = part.at[par, c_me, pl.ds(i * tiles * cols, tiles * cols)]
        return pltpu.make_async_remote_copy(
            src_ref=place, dst_ref=place,
            send_sem=chan_send.at[par, i, d], recv_sem=chan_recv.at[par, i, d],
            device_id={"chan": chan_peers[d]}, device_id_type=MESH,
        )

    def store_part(par, i, j, accs):
        for l in range(tiles):
            part[par, c_me, pl.ds((i * tiles + l) * cols + j, 1), :] = jnp.sum(
                accs[l], axis=0, keepdims=True
            )

    sides = []
    for da in (-1, 0, 1):
        for dx in (-1, 0, 1):
            if da == 0 and dx == 0:
                continue
            here = None
            for delta, me, count in ((da, a_me, n_along), (dx, x_me, n_across)):
                if delta:
                    ok = me > 0 if delta < 0 else me < count - 1
                    here = ok if here is None else jnp.logical_and(here, ok)
            if da and n_along == 1 or dx and n_across == 1:
                continue

            def span(delta, size):
                if delta == 0:
                    return WIDE, size, WIDE
                if delta < 0:
                    return WIDE, WIDE, WIDE + size
                return size, WIDE, 0

            sides.append((da, dx, here, span(da, rows), span(dx, cols)))

    def rim_copy(par, n):
        da, dx, _, (r0, rn, rt), (c0, cn, ct) = sides[n]
        return pltpu.make_async_remote_copy(
            src_ref=wide.at[par, pl.ds(r0, rn), pl.ds(c0 * PACK, cn * PACK)],
            dst_ref=wide.at[par, pl.ds(rt, rn), pl.ds(ct * PACK, cn * PACK)],
            send_sem=rim_send.at[par, n], recv_sem=rim_recv.at[par, n],
            device_id={"along": a_me + da, "across": x_me + dx}, device_id_type=MESH,
        )

    opposite = {
        n: next(m for m, t in enumerate(sides) if (t[0], t[1]) == (-s[0], -s[1]))
        for n, s in enumerate(sides)
    }

    def sum_copy(par, d):
        a, x = group_peers[d]
        place = sums.at[par, g_me]
        return pltpu.make_async_remote_copy(
            src_ref=place, dst_ref=place,
            send_sem=sum_send.at[par, d], recv_sem=sum_recv.at[par, d],
            device_id={"along": a, "across": x}, device_id_type=MESH,
        )

    def finish_chan(par):
        for i in range(rows):
            for d in range(n_chan - 1):
                chan_copy(par, i, d).wait_recv()
            for l in range(tiles):
                at = pl.ds((i * tiles + l) * cols, cols)
                total = part[par, 0, at, :]
                for c in range(1, n_chan):
                    total = total + part[par, c, at, :]
                wide[par, WIDE + i, pl.ds(WIDE * PACK + l, cols, stride=PACK), :] = total

    def start_rims(par):
        for n, side in enumerate(sides):
            @pl.when(side[2])
            def _():
                rim_copy(par, n).start()

    def finish_rims(par):
        for n, side in enumerate(sides):
            @pl.when(side[2])
            def _():
                rim_copy(par, opposite[n]).wait_recv()

    def finish_sends(par):
        for i in range(rows):
            for d in range(n_chan - 1):
                chan_copy(par, i, d).wait_send()
        for n, side in enumerate(sides):
            @pl.when(side[2])
            def _():
                rim_copy(par, n).wait_send()

    one, zero = jnp.float32(1), jnp.float32(0)
    row_edge = (
        jnp.where(a_me > 0, one, zero), jnp.where(a_me < n_along - 1, one, zero)
    )
    col_edge = (
        jnp.where(x_me > 0, one, zero), jnp.where(x_me < n_across - 1, one, zero)
    )
    pairs = ext_c // 2

    def spread_back_row(par, e):
        accs = [jnp.zeros((8, lanes), f32) for _ in range(pairs)]
        for a in range(TAPS):
            for b in range(TAPS):
                c = coef[a * TAPS + b]
                for g in range(pairs):
                    accs[g] = accs[g] + c * wide[
                        par, e + WIDE - a, pl.ds(8 * g + (WIDE - b) * PACK, 8), :
                    ]
        for g in range(pairs):
            scale = None
            if e < RIM or e >= RIM + rows:
                scale = row_edge[0 if e < RIM else 1]
            if g < RIM // 2 or g >= (RIM + cols) // 2:
                edge = col_edge[0 if g < RIM // 2 else 1]
                scale = edge if scale is None else scale * edge
            if scale is not None:
                accs[g] = accs[g] * scale
        return accs

    def spread_row(field, i):
        accs = [jnp.zeros((8, lanes), f32) for _ in range(cols // 2)]
        for a in range(TAPS):
            for b in range(TAPS):
                c = coef[a * TAPS + b]
                for g in range(cols // 2):
                    accs[g] = accs[g] + c * field[i + a, pl.ds(8 * g + b * PACK, 8), :]
        return accs

    for i in range(rows):
        loads[i].wait()
        for j in range(cols):
            f = i * cols + j
            flag = flag_ref[i, j].astype(f32)
            accs = [jnp.zeros((8, lanes), f32) for _ in range(tiles)]
            for k in range(blocks):
                z = jnp.broadcast_to(turned[k * 8 : (k + 1) * 8, f : f + 1], (8, lanes))
                for l in range(tiles):
                    accs[l] = accs[l] + z * jac[i, j, k * 8 : (k + 1) * 8, l * lanes : (l + 1) * lanes]
            store_part(0, i, j, [acc * flag for acc in accs])
        for d in range(n_chan - 1):
            chan_copy(0, i, d).start()
    finish_chan(0)
    start_rims(0)
    finish_rims(0)
    for e in range(ext_r):
        accs = spread_back_row(0, e)
        for g in range(pairs):
            fr[e, 8 * g : 8 * g + 8, :] = accs[g]
    finish_sends(0)

    def step(t, carry):
        par = lax.rem(t, 2)
        for i in range(rows):
            accs = spread_row(fr, i)
            for g in range(cols // 2):
                urs[i, 8 * g : 8 * g + 8, :] = accs[g]

            def column(j, carry):
                flag = flag_ref[i, j].astype(f32)
                x = [
                    jnp.broadcast_to(urs[i, pl.ds(j * PACK + l, 1), :] * flag, (8, lanes))
                    for l in range(tiles)
                ]
                accs = [jnp.zeros((8, lanes), f32) for _ in range(tiles)]
                for k in range(blocks):
                    js = [
                        jac[i, j, k * 8 : (k + 1) * 8, l * lanes : (l + 1) * lanes]
                        for l in range(tiles)
                    ]
                    y = js[0] * x[0]
                    for l in range(1, tiles):
                        y = y + js[l] * x[l]
                    z = jnp.sum(y, axis=1, keepdims=True) * wt[k]
                    for l in range(tiles):
                        accs[l] = accs[l] + js[l] * z
                store_part(par, i, j, accs)
                return carry

            lax.fori_loop(0, cols, column, 0, unroll=2)
            for d in range(n_chan - 1):
                chan_copy(par, i, d).start()

        norm_v = jnp.zeros((8, lanes), f32)
        for i in range(rows):
            for g in range(cols // 2):
                r = fr[RIM + i, 8 * g + RIM * PACK : 8 * g + RIM * PACK + 8, :]
                norm_v = norm_v + r * r
        finish_chan(par)
        start_rims(par)
        prod_v = norm_v
        for i in range(rows):
            for g in range(cols // 2):
                q = wide[par, WIDE + i, pl.ds(8 * g + WIDE * PACK, 8), :]
                prod_v = prod_v + urs[i, 8 * g : 8 * g + 8, :] * (
                    q
                )
        sums[par, g_me, 0:1, :] = jnp.sum(norm_v, axis=0, keepdims=True)
        sums[par, g_me, 1:2, :] = jnp.sum(prod_v, axis=0, keepdims=True)
        for d in range(group - 1):
            sum_copy(par, d).start()
        for d in range(group - 1):
            sum_copy(par, d).wait_recv()
        both = sums[par, 0]
        for n in range(1, group):
            both = both + sums[par, n]
        both = jnp.sum(both, axis=1, keepdims=True)
        fresh = jnp.broadcast_to(both[0:1], (8, lanes))
        product = jnp.broadcast_to(both[1:2], (8, lanes))
        beta = jnp.where(t == 1, zero, one) * (fresh / keep[0])
        alpha = fresh / (product - beta * fresh / keep[1])
        keep[0] = fresh
        keep[1] = alpha

        finish_rims(par)
        for e in range(ext_r):
            accs = spread_back_row(par, e)
            for g in range(pairs):
                at = slice(8 * g, 8 * g + 8)
                r = fr[e, at, :]
                d = r + beta * fd[e, at, :]
                c = (r + accs[g]) + beta * fc[e, at, :]
                fd[e, at, :] = d
                fc[e, at, :] = c
                fx[e, at, :] = fx[e, at, :] + alpha * d
                fr[e, at, :] = r - alpha * c
        finish_sends(par)
        for d in range(group - 1):
            sum_copy(par, d).wait_send()
        return carry

    lax.fori_loop(1, ITERS + 1, step, 0)

    for i in range(rows):
        accs = spread_row(fx, i)
        for g in range(cols // 2):
            urs[i, 8 * g : 8 * g + 8, :] = accs[g]
        for l in range(tiles):
            at = slice(l * lanes, (l + 1) * lanes)
            own = pl.ds(RIM * PACK + l, cols, stride=PACK)
            ctl_ref[i, :, at] = fx[RIM + i, own, :]
            res_ref[i, :, at] = fr[RIM + i, own, :]
            inc_ref[i, :, at] = urs[i, pl.ds(l, cols, stride=PACK), :]


def on_device(dims, jacobian, departures, inv_variance, channel_use, clear_flags, coefficients):
    rows, cols, chans, state = jacobian.shape
    lanes = 128
    n_along, n_across, n_chan = dims
    ext_r, ext_c = rows + 2 * RIM, cols + 2 * RIM
    field = jax.ShapeDtypeStruct((rows, cols, state), jnp.float32)
    vmem = pl.BlockSpec(memory_space=pltpu.VMEM)
    ext = pltpu.VMEM((ext_r, ext_c * PACK, lanes), jnp.float32)
    group = n_along * n_across
    return pl.pallas_call(
        functools.partial(kernel, dims),
        out_shape=(field, field, field),
        in_specs=[
            pl.BlockSpec(memory_space=pl.ANY), vmem, vmem, vmem,
            pl.BlockSpec(memory_space=pltpu.SMEM), vmem,
        ],
        out_specs=(vmem, vmem, vmem),
        scratch_shapes=[
            pltpu.VMEM((rows, cols, chans, state), jnp.float32),
            pltpu.VMEM((chans // 8, 8, lanes), jnp.float32),
            pltpu.VMEM((TAPS * TAPS, 8, lanes), jnp.float32),
            pltpu.VMEM((2, n_chan, rows * state // lanes * cols, lanes), jnp.float32),
            pltpu.VMEM((2, rows + 2 * WIDE, (cols + 2 * WIDE) * PACK, lanes), jnp.float32),
            pltpu.VMEM((2, group, 8, lanes), jnp.float32),
            pltpu.VMEM((rows, cols * PACK, lanes), jnp.float32),
            ext, ext, ext, ext,
            pltpu.VMEM((2, 8, lanes), jnp.float32),
            pltpu.SemaphoreType.DMA((rows,)),
            pltpu.SemaphoreType.DMA((2, rows, n_chan)),
            pltpu.SemaphoreType.DMA((2, rows, n_chan)),
            pltpu.SemaphoreType.DMA((2, 8)),
            pltpu.SemaphoreType.DMA((2, 8)),
            pltpu.SemaphoreType.DMA((2, group)),
            pltpu.SemaphoreType.DMA((2, group)),
        ],
        compiler_params=pltpu.CompilerParams(
            collective_id=0, has_side_effects=True, vmem_limit_bytes=40 * 1024 * 1024
        ),
    )(
        jacobian, departures, inv_variance.reshape(1, chans), channel_use.reshape(1, chans),
        clear_flags, coefficients,
    )


def solution(mesh):
    dims = (mesh.shape["along"], mesh.shape["across"], mesh.shape["chan"])
    return jax.shard_map(
        functools.partial(on_device, dims),
        mesh=mesh,
        in_specs=(
            P("along", "across", "chan", None),
            P("along", "across", "chan"),
            P("chan"),
            P("chan"),
            P("along", "across"),
            P(),
        ),
        out_specs=(
            P("along", "across", None),
            P("along", "across", None),
            P("along", "across", None),
        ),
        check_vma=False,
    )
```

time: 833 us -> 152 us (0.18)
  blocking collectives: 340 us -> 0 us
  starting transfers between devices: 189 us -> 0 us
  Pallas kernels: 0 us -> 142 us
  matrix products: 129 us -> 0 us
  waiting for transfers between devices: 122 us -> 0 us
  loops' own time: 31.3 us -> 0 us
  other arithmetic: 14.8 us -> 0 us
    psum x21 -> x0, blocking collectives: 340 us -> none  [the longest x11 192 us: back_project(): return lax.psum(adjoint_obs, 'chan')]
    ppermute x88 -> x0, starting transfers between devices: 189 us -> none  [the longest x44 130 us: extended(): lax.ppermute(tail, axis, [(i, (i + 1) % count) for i in range(ends)])]
    pallas_call x0 -> x1, Pallas kernels: none -> 142 us  [on_device(): pl.pallas_call(functools.partial(kernel, dims), out_shape=(field, field,...]
    dot_general x21 -> x0, matrix products: 129 us -> none  [the longest x10 87.2 us: forward(): jnp.einsum('xycs,xys->xyc', jacobian, field, precision=lax.Precision.HIGH...]
    ppermute x88 -> x0, waiting for transfers between devices: 122 us -> none  [the longest x44 111 us: extended(): lax.ppermute(head, axis, [((i + 1) % count, i) for i in range(ends)])]
    another operation x1 -> x0, loops' own time: 31.3 us -> none  [on_device(): lax.fori_loop(0, ITERS - 1, cg_step, (control, rhs, rhs, image, norm_now,...]
  transfers between devices with their start and end apart: 88 -> 0, of which waited for: 53 -> 0; matrix products, arithmetic and copies ran while one was open for 0% -> 0% of each run, Pallas kernels for 0% -> 0%
where the time goes in v1:
time: 152 us; the launch traced here: 151 us
  Pallas kernels  142 us (93%)
  local copies, waits for them, and re-layouts  8.14 us (5%)
    pallas_call x1, Pallas kernels, on_device(): pl.pallas_call(functools.partial(kernel, dims), out_shape=(field, field,...  142 us
    unnamed x15, local copies, waits for them, and re-layouts  8.14 us

profile of v1, /device:TPU:0, one launch (start us, length us, event | category | flops | bytes accessed | tf_op | source)
XLA Modules:
  0.0 151.2 jit_solution(3373478533464718931)
XLA Ops:
  0.6 0.0 copy-start
  0.6 2.8 %copy-done = f32[4,8,128,384]{3,2,1,0:T(8,128)S(1)} copy-done((f32[4,8,128,384]{3,2,1,0:T(8,128)S(1)}, f32[4,8,128,384]{3,2,1,0:T(8,128)}, u32[]{:S(2)}) %copy-start) | copy-done | bytes 6291480
  3.4 0.0 copy-start.1
  3.4 0.8 copy-done.1
  4.2 0.0 copy-start.2
  4.2 0.7 copy-done.2
  4.9 0.0 copy-start.3
  4.9 0.7 copy-done.3
  5.6 0.0 copy-start.4
  5.6 0.7 copy-done.4
  6.3 0.0 copy-start.5
  6.3 0.7 copy-done.5
  6.9 142.4 %shard_map.85 = (f32[4,8,384]{2,1,0:T(8,128)S(1)}, f32[4,8,384]{2,1,0:T(8,128)S(1)}, f32[4,8,384]{2,1,0:T(8,128)S(1)}) custom-call(f32[4,8,128,384]{3,2,1,0:T(8,128)S(1)} %copy-done, f32[4,8,128]{2,1,0:T(8,128)S(1)} %copy-done.2, f32[1,128]{1,0:T(1,128)S(1)} %bitcast.2, s32[1,128]{1,0:T(1,128)S(1)} %bitcast.3, s32[4,8]{1,0:T(4,128)S(1)} %copy-done.3, ...), custom_call_target="tpu_custom_call" | custom-call | tf_op jit(solution)/shard_map/pallas_call | solution.py:337
  149.3 0.6 copy.12
  150.0 0.6 copy.13
  150.6 0.6 copy.14
Async XLA Ops:
  0.6 2.8 %copy-start = (f32[4,8,128,384]{3,2,1,0:T(8,128)S(1)}, f32[4,8,128,384]{3,2,1,0:T(8,128)}, u32[]{:S(2)}) copy-start(f32[4,8,128,384]{3,2,1,0:T(8,128)} %jac_hbm.1) | copy-start | bytes 18874372
  3.4 0.8 copy-start.1
  4.2 0.7 copy-start.2
  4.9 0.7 copy-start.3
  5.6 0.7 copy-start.4
  6.3 0.7 copy-start.5

commit v2 on v1

--- a/solution.py
+++ b/solution.py
@@ -116,12 +116,12 @@
 
             sides.append((da, dx, here, span(da, rows), span(dx, cols)))
 
-    def rim_copy(par, n):
+    def rim_copy(par, n, k):
         da, dx, _, (r0, rn, rt), (c0, cn, ct) = sides[n]
         return pltpu.make_async_remote_copy(
-            src_ref=wide.at[par, pl.ds(r0, rn), pl.ds(c0 * PACK, cn * PACK)],
-            dst_ref=wide.at[par, pl.ds(rt, rn), pl.ds(ct * PACK, cn * PACK)],
-            send_sem=rim_send.at[par, n], recv_sem=rim_recv.at[par, n],
+            src_ref=wide.at[par, r0 + k, pl.ds(c0 * PACK, cn * PACK)],
+            dst_ref=wide.at[par, rt + k, pl.ds(ct * PACK, cn * PACK)],
+            send_sem=rim_send.at[par, n, k], recv_sem=rim_recv.at[par, n, k],
             device_id={"along": a_me + da, "across": x_me + dx}, device_id_type=MESH,
         )
 
@@ -149,18 +149,19 @@
                 for c in range(1, n_chan):
                     total = total + part[par, c, at, :]
                 wide[par, WIDE + i, pl.ds(WIDE * PACK + l, cols, stride=PACK), :] = total
-
-    def start_rims(par):
-        for n, side in enumerate(sides):
-            @pl.when(side[2])
-            def _():
-                rim_copy(par, n).start()
+            for n, side in enumerate(sides):
+                k = WIDE + i - side[3][0]
+                if 0 <= k < side[3][1]:
+                    @pl.when(side[2])
+                    def _():
+                        rim_copy(par, n, k).start()
 
     def finish_rims(par):
         for n, side in enumerate(sides):
             @pl.when(side[2])
             def _():
-                rim_copy(par, opposite[n]).wait_recv()
+                for k in range(sides[opposite[n]][3][1]):
+                    rim_copy(par, opposite[n], k).wait_recv()
 
     def finish_sends(par):
         for i in range(rows):
@@ -169,7 +170,8 @@
         for n, side in enumerate(sides):
             @pl.when(side[2])
             def _():
-                rim_copy(par, n).wait_send()
+                for k in range(side[3][1]):
+                    rim_copy(par, n, k).wait_send()
 
     one, zero = jnp.float32(1), jnp.float32(0)
     row_edge = (
@@ -223,7 +225,6 @@
         for d in range(n_chan - 1):
             chan_copy(0, i, d).start()
     finish_chan(0)
-    start_rims(0)
     finish_rims(0)
     for e in range(ext_r):
         accs = spread_back_row(0, e)
@@ -269,7 +270,6 @@
                 r = fr[RIM + i, 8 * g + RIM * PACK : 8 * g + RIM * PACK + 8, :]
                 norm_v = norm_v + r * r
         finish_chan(par)
-        start_rims(par)
         prod_v = norm_v
         for i in range(rows):
             for g in range(cols // 2):
@@ -355,13 +355,13 @@
             pltpu.SemaphoreType.DMA((rows,)),
             pltpu.SemaphoreType.DMA((2, rows, n_chan)),
             pltpu.SemaphoreType.DMA((2, rows, n_chan)),
-            pltpu.SemaphoreType.DMA((2, 8)),
-            pltpu.SemaphoreType.DMA((2, 8)),
+            pltpu.SemaphoreType.DMA((2, 8, max(rows, WIDE))),
+            pltpu.SemaphoreType.DMA((2, 8, max(rows, WIDE))),
             pltpu.SemaphoreType.DMA((2, group)),
             pltpu.SemaphoreType.DMA((2, group)),
         ],
         compiler_params=pltpu.CompilerParams(
-            collective_id=0, has_side_effects=True, vmem_limit_bytes=40 * 1024 * 1024
+            collective_id=0, has_side_effects=True, vmem_limit_bytes=60 * 1024 * 1024
         ),
     )(
         jacobian, departures, inv_variance.reshape(1, chans), channel_use.reshape(1, chans),

time: 152 us -> 135 us (0.89)
  Pallas kernels: 142 us -> 130 us
  local copies, waits for them, and re-layouts: 8.14 us -> 4.26 us
    pallas_call x1, Pallas kernels: 142 us -> 130 us  [on_device(): pl.pallas_call(functools.partial(kernel, dims), out_shape=(field, field,...]
    unnamed x15 -> x3, local copies, waits for them, and re-layouts: 8.14 us -> 4.26 us
where the time goes in v2:
time: 135 us; the launch traced here: 134 us
  Pallas kernels  130 us (96%)
  local copies, waits for them, and re-layouts  4.26 us (3%)
    pallas_call x1, Pallas kernels, on_device(): pl.pallas_call(functools.partial(kernel, dims), out_shape=(field, field,...  130 us
    unnamed x3, local copies, waits for them, and re-layouts  4.26 us

profile of v2, /device:TPU:0, one launch (start us, length us, event | category | flops | bytes accessed | tf_op | source)
XLA Modules:
  0.0 134.5 jit_solution(16566370754338170804)
XLA Ops:
  0.6 129.6 %shard_map.85 = (f32[4,8,384]{2,1,0:T(8,128)}, f32[4,8,384]{2,1,0:T(8,128)}, f32[4,8,384]{2,1,0:T(8,128)}) custom-call(f32[4,8,128,384]{3,2,1,0:T(8,128)} %jac_hbm.1, f32[4,8,128]{2,1,0:T(8,128)} %dep_ref.1, f32[1,128]{1,0:T(1,128)} %bitcast.2, s32[1,128]{1,0:T(1,128)} %bitcast.3, s32[4,8]{1,0:T(4,128)} %flag_ref.1, f32[25,384]{1,0:T(8,128)} %coef_ref.1), custom_call_target="tpu_custom_call" | custom-call | tf_op jit(solution)/shard_map/pallas_call | solution.py:337
  130.2 1.4 %copy.12 = f32[4,8,384]{2,1,0:T(8,128)} copy(f32[4,8,384]{2,1,0:T(8,128)} %get-tuple-element.6) | data formatting | bytes 98304
  131.6 1.4 %copy.13 = f32[4,8,384]{2,1,0:T(8,128)} copy(f32[4,8,384]{2,1,0:T(8,128)} %get-tuple-element.7) | data formatting | bytes 98304
  133.0 1.4 %copy.14 = f32[4,8,384]{2,1,0:T(8,128)} copy(f32[4,8,384]{2,1,0:T(8,128)} %get-tuple-element.8) | data formatting | bytes 98304

commit v3 on v2

--- a/solution.py
+++ b/solution.py
@@ -18,7 +18,7 @@
 def kernel(
     dims, jac_hbm, dep_ref, var_ref, use_ref, flag_ref, coef_ref,
     ctl_ref, inc_ref, res_ref,
-    jac, wt, coef, part, wide, sums, urs, fr, fd, fc, fx, keep,
+    jac, wt, coef, part, wide, sums, urs, image, fr, fd, fc, fx, keep,
     jac_sem, chan_send, chan_recv, rim_send, rim_recv, sum_send, sum_recv,
 ):
     n_along, n_across, n_chan = dims
@@ -260,7 +260,7 @@
                 store_part(par, i, j, accs)
                 return carry
 
-            lax.fori_loop(0, cols, column, 0, unroll=2)
+            lax.fori_loop(0, cols, column, 0, unroll=8)
             for d in range(n_chan - 1):
                 chan_copy(par, i, d).start()
 
@@ -274,15 +274,18 @@
         for i in range(rows):
             for g in range(cols // 2):
                 q = wide[par, WIDE + i, pl.ds(8 * g + WIDE * PACK, 8), :]
-                prod_v = prod_v + urs[i, 8 * g : 8 * g + 8, :] * (
-                    q
-                )
+                prod_v = prod_v + urs[i, 8 * g : 8 * g + 8, :] * q
         sums[par, g_me, 0:1, :] = jnp.sum(norm_v, axis=0, keepdims=True)
         sums[par, g_me, 1:2, :] = jnp.sum(prod_v, axis=0, keepdims=True)
         for d in range(group - 1):
             sum_copy(par, d).start()
+        finish_rims(par)
         for d in range(group - 1):
             sum_copy(par, d).wait_recv()
+        for e in range(ext_r):
+            accs = spread_back_row(par, e)
+            for g in range(pairs):
+                image[e, 8 * g : 8 * g + 8, :] = accs[g]
         both = sums[par, 0]
         for n in range(1, group):
             both = both + sums[par, n]
@@ -294,14 +297,12 @@
         keep[0] = fresh
         keep[1] = alpha
 
-        finish_rims(par)
         for e in range(ext_r):
-            accs = spread_back_row(par, e)
             for g in range(pairs):
                 at = slice(8 * g, 8 * g + 8)
                 r = fr[e, at, :]
                 d = r + beta * fd[e, at, :]
-                c = (r + accs[g]) + beta * fc[e, at, :]
+                c = (r + image[e, at, :]) + beta * fc[e, at, :]
                 fd[e, at, :] = d
                 fc[e, at, :] = c
                 fx[e, at, :] = fx[e, at, :] + alpha * d
@@ -350,7 +351,7 @@
             pltpu.VMEM((2, rows + 2 * WIDE, (cols + 2 * WIDE) * PACK, lanes), jnp.float32),
             pltpu.VMEM((2, group, 8, lanes), jnp.float32),
             pltpu.VMEM((rows, cols * PACK, lanes), jnp.float32),
-            ext, ext, ext, ext,
+            ext, ext, ext, ext, ext,
             pltpu.VMEM((2, 8, lanes), jnp.float32),
             pltpu.SemaphoreType.DMA((rows,)),
             pltpu.SemaphoreType.DMA((2, rows, n_chan)),

time: 135 us -> 128 us (0.948)
  Pallas kernels: 130 us -> 122 us
    pallas_call x1, Pallas kernels: 130 us -> 122 us  [on_device(): pl.pallas_call(functools.partial(kernel, dims), out_shape=(field, field,...]
where the time goes in v3:
time: 128 us; the launch traced here: 127 us
  Pallas kernels  122 us (95%)
  local copies, waits for them, and re-layouts  4.26 us (3%)
    pallas_call x1, Pallas kernels, on_device(): pl.pallas_call(functools.partial(kernel, dims), out_shape=(field, field,...  122 us
    unnamed x3, local copies, waits for them, and re-layouts  4.26 us

profile of v3, /device:TPU:0, one launch (start us, length us, event | category | flops | bytes accessed | tf_op | source)
XLA Modules:
  0.0 127.2 jit_solution(6116386516349188987)
XLA Ops:
  0.6 122.3 %shard_map.85 = (f32[4,8,384]{2,1,0:T(8,128)}, f32[4,8,384]{2,1,0:T(8,128)}, f32[4,8,384]{2,1,0:T(8,128)}) custom-call(f32[4,8,128,384]{3,2,1,0:T(8,128)} %jac_hbm.1, f32[4,8,128]{2,1,0:T(8,128)} %dep_ref.1, f32[1,128]{1,0:T(1,128)} %bitcast.2, s32[1,128]{1,0:T(1,128)} %bitcast.3, s32[4,8]{1,0:T(4,128)} %flag_ref.1, f32[25,384]{1,0:T(8,128)} %coef_ref.1), custom_call_target="tpu_custom_call" | custom-call | tf_op jit(solution)/shard_map/pallas_call | solution.py:338
  123.0 1.4 %copy.12 = f32[4,8,384]{2,1,0:T(8,128)} copy(f32[4,8,384]{2,1,0:T(8,128)} %get-tuple-element.6) | data formatting | bytes 98304
  124.4 1.4 %copy.13 = f32[4,8,384]{2,1,0:T(8,128)} copy(f32[4,8,384]{2,1,0:T(8,128)} %get-tuple-element.7) | data formatting | bytes 98304
  125.8 1.4 %copy.14 = f32[4,8,384]{2,1,0:T(8,128)} copy(f32[4,8,384]{2,1,0:T(8,128)} %get-tuple-element.8) | data formatting | bytes 98304

commit v4 on v3

--- a/solution.py
+++ b/solution.py
@@ -49,7 +49,8 @@
     coef[...] = jnp.zeros_like(coef)
     keep[...] = jnp.ones_like(keep)
 
-    chan_peers = [lax.rem(c_me + d, n_chan) for d in range(1, n_chan)]
+    steps = sorted(range(1, n_chan), key=lambda d: -min(d, n_chan - d))
+    chan_peers = [lax.rem(c_me + d, n_chan) for d in steps]
     group_peers = []
     for d in range(1, group):
         peer = lax.rem(g_me + d, group)
@@ -95,8 +96,8 @@
             )
 
     sides = []
-    for da in (-1, 0, 1):
-        for dx in (-1, 0, 1):
+    for dx in (-1, 1, 0):
+        for da in (-1, 0, 1):
             if da == 0 and dx == 0:
                 continue
             here = None

time: 128 us -> 129 us (level)
  Pallas kernels: 122 us -> 124 us
    pallas_call x1, Pallas kernels: 122 us -> 124 us  [on_device(): pl.pallas_call(functools.partial(kernel, dims), out_shape=(field, field,...]
where the time goes in v4:
time: 129 us
  Pallas kernels  124 us (96%)
  local copies, waits for them, and re-layouts  4.26 us (3%)
    pallas_call x1, Pallas kernels, on_device(): pl.pallas_call(functools.partial(kernel, dims), out_shape=(field, field,...  124 us
    unnamed x3, local copies, waits for them, and re-layouts  4.26 us

profile of v4, /device:TPU:0, one launch (start us, length us, event | category | flops | bytes accessed | tf_op | source)
XLA Modules:
  0.0 128.7 jit_solution(10261562547488573842)
XLA Ops:
  0.6 123.8 %shard_map.85 = (f32[4,8,384]{2,1,0:T(8,128)}, f32[4,8,384]{2,1,0:T(8,128)}, f32[4,8,384]{2,1,0:T(8,128)}) custom-call(f32[4,8,128,384]{3,2,1,0:T(8,128)} %jac_hbm.1, f32[4,8,128]{2,1,0:T(8,128)} %dep_ref.1, f32[1,128]{1,0:T(1,128)} %bitcast.2, s32[1,128]{1,0:T(1,128)} %bitcast.3, s32[4,8]{1,0:T(4,128)} %flag_ref.1, f32[25,384]{1,0:T(8,128)} %coef_ref.1), custom_call_target="tpu_custom_call" | custom-call | tf_op jit(solution)/shard_map/pallas_call | solution.py:339
  124.4 1.4 %copy.12 = f32[4,8,384]{2,1,0:T(8,128)} copy(f32[4,8,384]{2,1,0:T(8,128)} %get-tuple-element.6) | data formatting | bytes 98304
  125.9 1.4 %copy.13 = f32[4,8,384]{2,1,0:T(8,128)} copy(f32[4,8,384]{2,1,0:T(8,128)} %get-tuple-element.7) | data formatting | bytes 98304
  127.3 1.4 %copy.14 = f32[4,8,384]{2,1,0:T(8,128)} copy(f32[4,8,384]{2,1,0:T(8,128)} %get-tuple-element.8) | data formatting | bytes 98304
